TPU v7x, 256 devices: a whole 4x4x8 slice. The times are simulated.
256 devices in a mesh: gx: 16 (over z, core), gy: 16 (over y, x).
Axes of the slice: x: 4, y: 4, z: 8, core: 2. Of those that a mesh axis runs over, the one named last changes fastest.
Arguments:
- modes: float32 [524288, 512], P(('gx', 'gy'))
- batch: float32 [524288, 256], P(('gx', 'gy')), as said below
- core: float32 [768, 512], replicated, may hold values from -0.21875 to 0.21875
Outputs:
- new_modes: float32 [524288, 512], P(('gx', 'gy'))
Inputs may be any that keep to these rules, and one draw needn't show every extreme that they name: Each row of modes and batch shares one positive scale; batch holds a sizeable part of the span of modes.
All inputs are finite; a program needn't handle non-finite values.
Results may differ from a plain program's by a relative error of at most 0.000058.
Values sent between devices are 32-bit elements; how exact they have to be, the bound alone decides.
A program may use at most 64 MiB of HBM per device.

v0:
```python
import jax
import jax.numpy as jnp
from jax import lax
from jax.sharding import PartitionSpec as P


def matmul(left, right):
    return jnp.dot(left, right, precision=lax.Precision.HIGHEST, preferred_element_type=jnp.float32)


def global_sum(parts):
    return lax.psum((parts[0],), ("gx", "gy"))


def shards(modes, batch, core):
    total_rows = modes.shape[0] * lax.axis_size("gx") * lax.axis_size("gy")
    width = modes.shape[1]
    top = matmul(modes, core[:width])
    cross = global_sum((matmul(modes.T, batch),))[0]
    coeffs = cross / total_rows
    resid = batch - matmul(modes, coeffs)
    gram = global_sum((matmul(resid.T, resid),))[0] / total_rows
    lower = jnp.linalg.cholesky(gram)
    basis = jax.scipy.linalg.solve_triangular(lower, resid.T, lower=True).T
    return top + matmul(basis, core[width:])


def solution(mesh):
    placed = (P(("gx", "gy"), None), P(("gx", "gy"), None), P())
    return jax.shard_map(
        shards, mesh=mesh, in_specs=placed, out_specs=P(("gx", "gy"), None), check_vma=False
    )
```

profile of v0, /device:TPU:2, one launch (start us, length us, event | category | flops | bytes accessed | tf_op | source)
XLA Modules:
  0.0 619.7 jit_solution(16031329301337902461)
XLA Ops:
  6.5 0.0 copy-start.1
  6.5 0.0 all-reduce.4.cloned.1.call-start
  6.5 10.5 %fusion.20 = f32[512,256]{1,0:T(8,128)} fusion(f32[2048,512]{1,0:T(8,128)} %param.3, f32[2048,256]{1,0:T(8,128)} %param.4), kind=kOutput, calls=%fused_computation.42 | convolution fusion | flops 3221225472 | bytes 6815744 | tf_op jit(solution)/shard_map/dot_general | solution.py:8
  17.0 0.0 all-reduce.4.cloned.1.call-update
  17.0 0.5 all-reduce.6.cloned.1.call-start
  17.6 0.0 copy-done.1
  17.6 1.8 copy.4
  19.4 256.1 %all-reduce.4.cloned.1.call-done = f32[512,256]{1,0:T(8,128)} async-done(((f32[512,256]{1,0:T(8,128)}), f32[512,256]{1,0:T(8,128)}) %all-reduce.4.cloned.1.call-update) | async-done | bytes 524304 | tf_op jit(solution)/shard_map/psum | solution.py:12
  275.5 9.9 %fusion = f32[2048,256]{0,1:T(8,128)S(1)} fusion(f32[2048,256]{0,1:T(8,128)} %copy.4, f32[2048,512]{1,0:T(8,128)} %param.3, f32[512,256]{1,0:T(8,128)} %all-reduce.4.cloned.1.call-done), kind=kOutput, calls=%fused_computation.4 | convolution fusion | flops 3221880832 | bytes 8912896 | tf_op jit(solution)/shard_map/dot_general | solution.py:8
  285.5 2.6 fusion.21
  288.0 0.0 all-reduce.6.cloned.1.call-update
  288.1 10.2 %fusion.6 = f32[2048,512]{1,0:T(8,128)} fusion(f32[2048,512]{1,0:T(8,128)} %param.3, f32[768,512]{1,0:T(8,128)} %param.5), kind=kOutput, calls=%fused_computation.12 | convolution fusion | flops 6442450944 | bytes 9437184 | tf_op jit(solution)/shard_map/dot_general | solution.py:8
  298.3 242.9 %all-reduce.6.cloned.1.call-done = f32[256,256]{0,1:T(8,128)} async-done(((f32[256,256]{0,1:T(8,128)}), f32[256,256]{0,1:T(8,128)}) %all-reduce.6.cloned.1.call-update) | async-done | bytes 262160 | tf_op jit(solution)/shard_map/psum | solution.py:12
  541.2 1.0 broadcast_multiply_fusion
  542.2 0.1 copy.6
  542.3 1.0 fusion.10
  543.3 11.7 %cholesky.50 = f32[128,128]{1,0:T(8,128)S(1)} custom-call(f32[128,128]{1,0:T(8,128)S(1)} %cholesky.118), custom_call_target="Cholesky" | custom-call | tf_op jit(solution)/shard_map/jit(cholesky)/cholesky | solution.py:23
  555.0 9.8 %custom-call.15 = f32[1,128,128]{1,2,0:T(8,128)S(1)} custom-call(f32[1,128,128]{2,1,0:T(8,128)S(1)} %get-tuple-element.26), custom_call_target="InvertDiagBlocksLowerTriangular" | custom-call | tf_op jit(solution)/shard_map/jit(cholesky)/cholesky | solution.py:23
  564.9 0.2 constant_dynamic-update-slice_fusion.1
  565.1 0.3 convolution_subtract_fusion.1
  565.4 11.7 %cholesky.105 = f32[128,128]{1,0:T(8,128)S(1)} custom-call(f32[128,128]{1,0:T(8,128)S(1)} %convolution_subtract_fusion.1), custom_call_target="Cholesky" | custom-call | tf_op jit(solution)/shard_map/jit(cholesky)/cholesky | solution.py:23
  577.1 0.7 compare_reduce_fusion
  579.1 0.1 triangular_solve.57
  579.2 4.1 while.1
  579.2 0.7 fusion.33
  579.9 1.3 bitcast_dynamic-update-slice_fusion.2
  581.2 0.7 fusion.33
  581.9 1.3 bitcast_dynamic-update-slice_fusion.2
  583.3 19.9 %custom-call.16 = f32[2,128,128]{1,2,0:T(8,128)S(1)} custom-call(f32[2,128,128]{2,1,0:T(8,128)S(1)} %get-tuple-element.12), custom_call_target="InvertDiagBlocksLowerTriangular" | custom-call | tf_op jit(solution)/shard_map/jit(_solve_triangular)/triangular_solve | solution.py:24
  603.2 1.1 fusion.4
  604.2 0.0 copy-start
  604.2 1.0 convolution_subtract_fusion
  605.2 1.1 fusion.13
  606.3 0.1 copy-done
  606.4 6.2 %convolution_add_fusion = f32[2048,512]{1,0:T(8,128)} fusion(f32[2048,512]{1,0:T(8,128)S(1)} %copy-done, f32[128,2048]{1,0:T(8,128)S(1)} %fusion.13, f32[128,2048]{1,0:T(8,128)S(1)} %fusion.4, f32[768,512]{1,0:T(8,128)} %param.5), kind=kOutput, calls=%fused_computation.2 | convolution fusion | flops 3222798336 | bytes 11010048 | tf_op jit(solution)/shard_map/dot_general | solution.py:8
  (9 shorter events, 0.1 us)
Async XLA Ops:
  6.5 11.0 %copy-start.1 = (f32[2048,256]{1,0:T(8,128)S(1)}, f32[2048,256]{1,0:T(8,128)}, u32[]{:S(2)}) copy-start(f32[2048,256]{1,0:T(8,128)} %param.4) | copy-start | bytes 6291460
  6.5 269.0 %all-reduce.4.cloned.1.call-start = ((), (), s32[]{:S(2)}) async-start(), calls=%async_computation | async-start | bytes 1048576 | tf_op jit(solution)/shard_map/psum | solution.py:12
  17.0 524.1 %all-reduce.6.cloned.1.call-start = ((), (), s32[]{:S(2)}) async-start(), calls=%async_computation.1 | async-start | bytes 524288 | tf_op jit(solution)/shard_map/psum | solution.py:12
  604.2 2.2 copy-start
Sparse Core Ops, SparseCore 0:
  17.2 258.3 all-reduce.3
  288.2 252.9 all-reduce.5
where the time goes:
time: 625 us; the launch traced here: 620 us
  waiting for transfers between devices  499 us (80%)
  other arithmetic  55.9 us (9%)
  matrix products  43 us (7%)
  between operations  15 us (2%)
    psum x2, waiting for transfers between devices, global_sum(): return lax.psum((parts[0],), ('gx', 'gy'))  499 us
    dot_general x5, matrix products, matmul(): jnp.dot(left, right, precision=lax.Precision.HIGHEST, preferred_element_t...  39.5 us
    another operation x6, other arithmetic, shards(): lower = jnp.linalg.cholesky(gram)  34 us
    another operation x3, other arithmetic, shards(): basis = jax.scipy.linalg.solve_triangular(lower, resid.T, lower=True).T  19.9 us
  transfers between devices with their start and end apart: 2, of which 2 were waited for; matrix products, arithmetic and copies ran while one was open for 2% of the time, Pallas kernels for 0%

commit v1 on v0

--- a/solution.py
+++ b/solution.py
@@ -9,7 +9,7 @@
 
 
 def global_sum(parts):
-    return lax.psum((parts[0],), ("gx", "gy"))
+    return lax.psum(lax.psum((parts[0],), "gy"), "gx")
 
 
 def shards(modes, batch, core):

time: 625 us -> 532 us (0.85)
  waiting for transfers between devices: 499 us -> 406 us
    psum x2 -> x4, waiting for transfers between devices: 499 us -> 406 us  [global_sum(): return lax.psum(lax.psum((parts[0],), 'gy'), 'gx')]
  transfers between devices with their start and end apart: 2 -> 4, of which waited for: 2 -> 4; matrix products, arithmetic and copies ran while one was open for 2% -> 2% of each run, Pallas kernels for 0% -> 0%
where the time goes in v1:
time: 532 us; the launch traced here: 526 us
  waiting for transfers between devices  406 us (76%)
  other arithmetic  55.9 us (11%)
  matrix products  43 us (8%)
  between operations  14.8 us (3%)
  local copies, waits for them, and re-layouts  6.17 us (1%)
    psum x4, waiting for transfers between devices, global_sum(): return lax.psum(lax.psum((parts[0],), 'gy'), 'gx')  406 us
    dot_general x5, matrix products, matmul(): jnp.dot(left, right, precision=lax.Precision.HIGHEST, preferred_element_t...  39.4 us
    another operation x6, other arithmetic, shards(): lower = jnp.linalg.cholesky(gram)  34 us
    another operation x3, other arithmetic, shards(): basis = jax.scipy.linalg.solve_triangular(lower, resid.T, lower=True).T  19.9 us
  transfers between devices with their start and end apart: 4, of which 4 were waited for; matrix products, arithmetic and copies ran while one was open for 2% of the time, Pallas kernels for 0%

profile of v1, /device:TPU:2, one launch (start us, length us, event | category | flops | bytes accessed | tf_op | source)
XLA Modules:
  0.0 526.3 jit_solution(12167794753438697266)
XLA Ops:
  6.5 0.0 all-reduce.6.cloned.1.call-start
  6.5 0.0 copy-start.1
  6.5 10.5 %fusion.20 = f32[512,256]{1,0:T(8,128)} fusion(f32[2048,512]{1,0:T(8,128)} %param.3, f32[2048,256]{1,0:T(8,128)} %param.4), kind=kOutput, calls=%fused_computation.42 | convolution fusion | flops 3221225472 | bytes 6815744 | tf_op jit(solution)/shard_map/dot_general | solution.py:8
  17.0 0.0 all-reduce.6.cloned.1.call-update
  17.0 0.0 all-reduce.8.cloned.1.call-start
  17.1 98.5 %all-reduce.6.cloned.1.call-done = f32[512,256]{1,0:T(8,128)} async-done(((f32[512,256]{1,0:T(8,128)}), f32[512,256]{1,0:T(8,128)}) %all-reduce.6.cloned.1.call-update) | async-done | bytes 524304 | tf_op jit(solution)/shard_map/psum | solution.py:12
  115.6 0.0 all-reduce.8.cloned.1.call-update
  115.6 0.5 all-reduce.10.cloned.1.call-start
  116.1 0.0 copy-done.1
  116.1 1.8 copy.4
  117.9 110.4 %all-reduce.8.cloned.1.call-done = f32[512,256]{1,0:T(8,128)} async-done(((f32[512,256]{1,0:T(8,128)}), f32[512,256]{1,0:T(8,128)}) %all-reduce.8.cloned.1.call-update) | async-done | bytes 524304 | tf_op jit(solution)/shard_map/psum | solution.py:12
  228.3 9.9 %fusion = f32[2048,256]{0,1:T(8,128)S(1)} fusion(f32[2048,256]{0,1:T(8,128)} %copy.4, f32[2048,512]{1,0:T(8,128)} %param.3, f32[512,256]{1,0:T(8,128)} %all-reduce.8.cloned.1.call-done), kind=kOutput, calls=%fused_computation.4 | convolution fusion | flops 3221880832 | bytes 8912896 | tf_op jit(solution)/shard_map/dot_general | solution.py:8
  238.3 2.6 fusion.21
  240.8 0.0 all-reduce.10.cloned.1.call-update
  240.9 0.0 all-reduce.12.cloned.1.call-start
  240.9 95.2 %all-reduce.10.cloned.1.call-done = f32[256,256]{0,1:T(8,128)} async-done(((f32[256,256]{0,1:T(8,128)}), f32[256,256]{0,1:T(8,128)}) %all-reduce.10.cloned.1.call-update) | async-done | bytes 262160 | tf_op jit(solution)/shard_map/psum | solution.py:12
  336.1 0.0 all-reduce.12.cloned.1.call-update
  336.1 10.2 %fusion.6 = f32[2048,512]{1,0:T(8,128)} fusion(f32[2048,512]{1,0:T(8,128)} %param.3, f32[768,512]{1,0:T(8,128)} %param.5), kind=kOutput, calls=%fused_computation.12 | convolution fusion | flops 6442450944 | bytes 9437184 | tf_op jit(solution)/shard_map/dot_general | solution.py:8
  346.4 101.7 %all-reduce.12.cloned.1.call-done = f32[256,256]{0,1:T(8,128)} async-done(((f32[256,256]{0,1:T(8,128)}), f32[256,256]{0,1:T(8,128)}) %all-reduce.12.cloned.1.call-update) | async-done | bytes 262160 | tf_op jit(solution)/shard_map/psum | solution.py:12
  448.1 1.0 broadcast_multiply_fusion
  449.0 0.1 copy.6
  449.2 1.0 fusion.10
  450.2 11.7 %cholesky.50 = f32[128,128]{1,0:T(8,128)S(1)} custom-call(f32[128,128]{1,0:T(8,128)S(1)} %cholesky.118), custom_call_target="Cholesky" | custom-call | tf_op jit(solution)/shard_map/jit(cholesky)/cholesky | solution.py:23
  461.9 9.8 %custom-call.15 = f32[1,128,128]{1,2,0:T(8,128)S(1)} custom-call(f32[1,128,128]{2,1,0:T(8,128)S(1)} %get-tuple-element.26), custom_call_target="InvertDiagBlocksLowerTriangular" | custom-call | tf_op jit(solution)/shard_map/jit(cholesky)/cholesky | solution.py:23
  471.8 0.2 constant_dynamic-update-slice_fusion.1
  472.0 0.3 convolution_subtract_fusion.1
  472.2 11.7 %cholesky.105 = f32[128,128]{1,0:T(8,128)S(1)} custom-call(f32[128,128]{1,0:T(8,128)S(1)} %convolution_subtract_fusion.1), custom_call_target="Cholesky" | custom-call | tf_op jit(solution)/shard_map/jit(cholesky)/cholesky | solution.py:23
  484.0 0.7 compare_reduce_fusion
  486.0 0.1 triangular_solve.57
  486.1 4.1 while.1
  486.1 0.7 fusion.33
  486.8 1.3 bitcast_dynamic-update-slice_fusion.2
  488.1 0.7 fusion.33
  488.8 1.3 bitcast_dynamic-update-slice_fusion.2
  490.1 19.9 %custom-call.16 = f32[2,128,128]{1,2,0:T(8,128)S(1)} custom-call(f32[2,128,128]{2,1,0:T(8,128)S(1)} %get-tuple-element.12), custom_call_target="InvertDiagBlocksLowerTriangular" | custom-call | tf_op jit(solution)/shard_map/jit(_solve_triangular)/triangular_solve | solution.py:24
  510.0 1.1 fusion.4
  511.1 0.0 copy-start
  511.1 1.0 convolution_subtract_fusion
  512.1 1.1 fusion.13
  513.2 0.1 copy-done
  513.3 6.2 %convolution_add_fusion = f32[2048,512]{1,0:T(8,128)} fusion(f32[2048,512]{1,0:T(8,128)S(1)} %copy-done, f32[128,2048]{1,0:T(8,128)S(1)} %fusion.13, f32[128,2048]{1,0:T(8,128)S(1)} %fusion.4, f32[768,512]{1,0:T(8,128)} %param.5), kind=kOutput, calls=%fused_computation.2 | convolution fusion | flops 3222798336 | bytes 11010048 | tf_op jit(solution)/shard_map/dot_general | solution.py:8
  (9 shorter events, 0.1 us)
Async XLA Ops:
  6.5 109.1 %all-reduce.6.cloned.1.call-start = ((), (), s32[]{:S(2)}) async-start(), calls=%async_computation | async-start | bytes 1048576 | tf_op jit(solution)/shard_map/psum | solution.py:12
  6.5 109.6 %copy-start.1 = (f32[2048,256]{1,0:T(8,128)S(1)}, f32[2048,256]{1,0:T(8,128)}, u32[]{:S(2)}) copy-start(f32[2048,256]{1,0:T(8,128)} %param.4) | copy-start | bytes 6291460
  17.0 211.3 %all-reduce.8.cloned.1.call-start = ((), (), s32[]{:S(2)}) async-start(), calls=%async_computation.1 | async-start | bytes 1048576 | tf_op jit(solution)/shard_map/psum | solution.py:12
  115.6 220.5 %all-reduce.10.cloned.1.call-start = ((), (), s32[]{:S(2)}) async-start(), calls=%async_computation.2 | async-start | bytes 524288 | tf_op jit(solution)/shard_map/psum | solution.py:12
  240.9 207.2 %all-reduce.12.cloned.1.call-start = ((), (), s32[]{:S(2)}) async-start(), calls=%async_computation.3 | async-start | bytes 524288 | tf_op jit(solution)/shard_map/psum | solution.py:12
  511.1 2.2 copy-start
Sparse Core Ops, SparseCore 0:
  17.1 98.4 all-reduce.5
  117.9 110.3 all-reduce.7
  241.0 95.0 all-reduce.9
  338.3 109.7 all-reduce.11
